TPU v7x, 32 devices: a whole 2x2x4 slice. The times are simulated.
32 devices in a mesh: tm: 2 (over y), rows: 4 (over z), dp: 4 (over x, core).
Axes of the slice: x: 2, y: 2, z: 4, core: 2. Of those that a mesh axis runs over, the one named last changes fastest.
Arguments:
- video: bfloat16 [4, 32, 16, 32, 128], P('dp', 'tm', 'rows'), may hold values from -6 to 6
- cotangent: bfloat16 [4, 32, 16, 32, 128], P('dp', 'tm', 'rows'), may hold values from -6 to 6
- in_kernel: bfloat16 [3, 3, 128, 128], replicated, may hold values from -0.03125 to 0.03125
- out_kernel: bfloat16 [3, 3, 128, 128], replicated, may hold values from -0.1875 to 0.1875
- skip_gain: float32 [128], replicated, may hold values from 0.5 to 1.5
- log_decay: float32 [32, 128], P('tm'), may hold values from -3 to 0, as said below
Outputs:
- layer_out: bfloat16 [4, 32, 16, 32, 128], P('dp', 'tm', 'rows')
- video_grad: bfloat16 [4, 32, 16, 32, 128], P('dp', 'tm', 'rows')
- in_kernel_grad: float32 [3, 3, 128, 128], replicated
- out_kernel_grad: float32 [3, 3, 128, 128], replicated
- skip_gain_grad: float32 [128], replicated
- decay_grad: float32 [32, 128], P('tm')
Inputs may be any that keep to these rules, and one draw needn't show every extreme that they name: log_decay is negative.
All inputs are finite; a program needn't handle non-finite values.
Results may differ from a plain program's by a relative error of at most 0.0085.
Values may be sent and summed in bfloat16 or wider, within the bound.
No kernel may reach another device: no remote copies, remote signals or barrier semaphores. Data moves between devices by JAX's collectives and lax.ppermute only.
A program may use at most 64 MiB of HBM per device.

v0:
```python
import math
import jax
import jax.numpy as jnp
from jax import lax
from jax.sharding import PartitionSpec as P


def padded_2(cells, sides, width):
    for axis, dim in sides:
        count = lax.axis_size(axis)
        ends = count - 1
        head = lax.slice_in_dim(cells, 0, width, axis=dim)
        tail = lax.slice_in_dim(cells, cells.shape[dim] - width, cells.shape[dim], axis=dim)
        cells = jnp.concatenate(
            [
                lax.ppermute(tail, axis, [(i, (i + 1) % count) for i in range(ends)]),
                cells,
                lax.ppermute(head, axis, [((i + 1) % count, i) for i in range(ends)]),
            ],
            axis=dim,
        )
    return cells


def pad_columns(field):
    return jnp.pad(field, ((0, 0), (0, 0), (0, 0), (1, 1), (0, 0)))


def forward_conv(padded, kernel):
    seqs, frames, rows_two, cols_two, chans = padded.shape
    rows, cols = (rows_two - 2, cols_two - 2)
    total = None
    for i in range(3):
        for j in range(3):
            piece = padded[:, :, i : i + rows, j : j + cols, :].reshape(-1, chans)
            term = jnp.dot(piece, kernel[i, j], preferred_element_type=jnp.float32)
            total = term if total is None else total + term
    return total.reshape(seqs, frames, rows, cols, kernel.shape[3])


def adjoint_conv(padded, kernel):
    seqs, frames, rows_two, cols_two, chans = padded.shape
    rows, cols = (rows_two - 2, cols_two - 2)
    total = None
    for i in range(3):
        for j in range(3):
            piece = padded[:, :, 2 - i : 2 - i + rows, 2 - j : 2 - j + cols, :].reshape(-1, chans)
            term = lax.dot_general(
                piece, kernel[i, j], (((1,), (1,)), ((), ())), preferred_element_type=jnp.float32
            )
            total = term if total is None else total + term
    return total.reshape(seqs, frames, rows, cols, kernel.shape[2])


def kernel_grad(padded, grad):
    seqs, frames, rows_two, cols_two, chans = padded.shape
    rows, cols = (rows_two - 2, cols_two - 2)
    flat_grad = grad.reshape(-1, grad.shape[-1])
    outer_list = []
    for i in range(3):
        inner_list = []
        for j in range(3):
            piece = padded[:, :, i : i + rows, j : j + cols, :].reshape(-1, chans)
            inner_list.append(
                lax.dot_general(
                    piece, flat_grad, (((0,), (0,)), ((), ())), preferred_element_type=jnp.float32
                )
            )
        outer_list.append(jnp.stack(inner_list))
    return jnp.stack(outer_list)


def on_device(video, cotangent, in_kernel, out_kernel, skip_gain, log_decay):
    seqs, frames, rows, cols, chans = video.shape
    padded_x = pad_columns(padded_2(video, (("rows", 2),), 1))
    drive = forward_conv(padded_x, in_kernel)
    cum = jnp.cumsum(log_decay, axis=0)
    later_mask = (
        lax.broadcasted_iota(jnp.int32, (frames, frames), 0)
        >= lax.broadcasted_iota(jnp.int32, (frames, frames), 1)
    )[:, :, None]
    gaps = cum[:, None, :] - cum[None, :, :]
    within = jnp.where(later_mask, jnp.exp(jnp.where(later_mask, gaps, 0.0)), 0.0)
    local_states = jnp.einsum("tkp,skrcp->strcp", within, drive, precision=lax.Precision.HIGHEST)
    group_total = cum[-1]
    empty = jnp.zeros_like(local_states[:, -1])
    group_logs = lax.all_gather(group_total[None, :], "tm", axis=0, tiled=True)
    running = jnp.cumsum(group_logs, axis=0)
    own = lax.axis_index("tm")
    own_running = lax.dynamic_index_in_dim(running, own, 0, keepdims=False)
    piece = lax.all_gather(
        local_states[:, -1][None].astype(jnp.bfloat16), "tm", axis=0, tiled=True
    ).astype(jnp.float32)
    count = piece.shape[0]
    upto = running
    index = jnp.arange(count, dtype=jnp.int32)
    reach = own_running[None, :] - group_total[None, :] - upto
    weight = jnp.where((index < own)[:, None], jnp.exp(jnp.minimum(reach, 0.0)), 0.0)
    carry_in = empty + jnp.einsum("np,nsrcp->srcp", weight, piece, precision=lax.Precision.HIGHEST)
    states = local_states + jnp.exp(cum)[None, :, None, None, :] * carry_in[:, None]
    states_bf = states.astype(jnp.bfloat16)
    padded_s = pad_columns(padded_2(states_bf, (("rows", 2),), 1))
    pre = forward_conv(padded_s, out_kernel) + skip_gain * video.astype(jnp.float32)
    activated, pullback = jax.vjp(jax.nn.gelu, pre)
    grad_pre = pullback(cotangent.astype(jnp.float32))[0]
    grad_bf = grad_pre.astype(jnp.bfloat16)
    out_grad = kernel_grad(padded_s, grad_bf)
    gain_grad = jnp.sum(grad_pre * video.astype(jnp.float32), axis=(0, 1, 2, 3))
    padded_g = pad_columns(padded_2(grad_bf, (("rows", 2),), 1))
    state_grad = adjoint_conv(padded_g, out_kernel)
    local_adjoint = jnp.einsum(
        "tkp,strcp->skrcp", within, state_grad, precision=lax.Precision.HIGHEST
    )
    leading = jnp.exp(cum[0])[None, None, None, :] * local_adjoint[:, 0]
    piece = lax.all_gather(leading[None].astype(jnp.bfloat16), "tm", axis=0, tiled=True).astype(
        jnp.float32
    )
    count = piece.shape[0]
    upto = running
    index = jnp.arange(count, dtype=jnp.int32)
    reach = upto - group_logs - own_running[None, :]
    weight = jnp.where((index > own)[:, None], jnp.exp(jnp.minimum(reach, 0.0)), 0.0)
    back_in = empty + jnp.einsum("np,nsrcp->srcp", weight, piece, precision=lax.Precision.HIGHEST)
    adjoint = (
        local_adjoint
        + jnp.exp(group_total[None, :] - cum)[None, :, None, None, :] * back_in[:, None]
    )
    previous = jnp.concatenate([carry_in[:, None], states[:, :-1]], axis=1)
    decay_part = jnp.sum(
        adjoint * jnp.exp(log_decay)[None, :, None, None, :] * previous, axis=(0, 2, 3)
    )
    decay_scale = 1.0 / math.sqrt(seqs * rows * cols * lax.axis_size("rows") * lax.axis_size("dp"))
    decay_grad = lax.psum(decay_part, ("rows", "dp")) * decay_scale
    adjoint_bf = adjoint.astype(jnp.bfloat16)
    in_grad = kernel_grad(padded_x, adjoint_bf)
    padded_a = pad_columns(padded_2(adjoint_bf, (("rows", 2),), 1))
    video_grad = (adjoint_conv(padded_a, in_kernel) + skip_gain * grad_pre).astype(jnp.bfloat16)
    in_sum, out_sum, gain_sum = lax.psum((in_grad, out_grad, gain_grad), ("tm", "rows", "dp"))
    weight_scale = 1.0 / math.sqrt(
        seqs
        * frames
        * rows
        * cols
        * lax.axis_size("tm")
        * lax.axis_size("rows")
        * lax.axis_size("dp")
    )
    return (
        activated.astype(jnp.bfloat16),
        video_grad,
        in_sum * weight_scale,
        out_sum * weight_scale,
        gain_sum * weight_scale,
        decay_grad,
    )


def solution(mesh):
    placed = (
        P("dp", "tm", "rows", None, None),
        P("dp", "tm", "rows", None, None),
        P(),
        P(),
        P(),
        P("tm", None),
    )
    return jax.shard_map(
        on_device,
        mesh=mesh,
        in_specs=placed,
        out_specs=(
            P("dp", "tm", "rows", None, None),
            P("dp", "tm", "rows", None, None),
            P(),
            P(),
            P(),
            P("tm", None),
        ),
        check_vma=False,
    )
```

profile of v0, /device:TPU:0, one launch (start us, length us, event | category | flops | bytes accessed | tf_op | source)
XLA Modules:
  0.0 367.8 jit_solution(14901978521855251328)
XLA Ops:
  7.2 1.0 fusion.177
  8.2 5.0 %collective-permute-start = (bf16[1,16,1,32,128]{4,3,2,1,0:T(8,128)(2,1)S(1)}, bf16[1,16,1,32,128]{4,3,2,1,0:T(8,128)(2,1)S(1)}, u32[]{:S(2)}, u32[]{:S(2)}) collective-permute-start(bf16[1,16,1,32,128]{4,3,2,1,0:T(8,128)(2,1)S(1)} %get-tuple-element.71), channel_id=1, source_target_pairs={{0,4},{4,8},{8,12},{1,5},{5,9},{9,13},{2,6},{6,10},{10,14},{3,7},{... | collective-permute-start | bytes 393224 | tf_op jit(solution)/shard_map/ppermute | solution.py:16
  13.2 1.3 collective-permute-start.1
  15.2 4.2 %all-gather = f32[2,1,128]{2,1,0:T(1,128)S(1)} all-gather(f32[1,1,128]{2,1,0:T(1,128)S(1)} %slice_bitcast_fusion.1), channel_id=1, replica_groups=mesh['tm'=2,'rows'=4,'dp'=4] {'tm'}, dimensions={0}, use_global_device_ids=true | all-gather | bytes 1536 | tf_op jit(solution)/shard_map/all_gather | solution.py:87
  20.0 1.6 fusion.25
  25.6 4.5 %copy.169 = f32[16,4,32,128]{2,0,1,3:T(8,128)} copy(f32[16,4,32,128]{3,2,1,0:T(8,128)S(1)} %bitcast.443) | data formatting | bytes 2097152 | tf_op jit(solution)/shard_map/reshape
  30.1 8.3 %fusion.19 = f32[128,4,32,16]{2,3,1,0:T(8,128)} fusion(f32[16,4,32,128]{2,0,1,3:T(8,128)} %copy.169, f32[16,128]{0,1:T(8,128)S(1)} %copy.167, pred[16,16]{0,1:T(8,128)(4,1)S(1)} %iota_compare_fusion.2), kind=kOutput, calls=%fused_computation.74 | convolution fusion | flops 50429952 | bytes 2105600 | tf_op jit(solution)/shard_map/tkp,skrcp->strcp/dot_general | solution.py:84
  38.4 3.7 %copy.171 = f32[128,4,32,16]{0,2,1,3:T(8,128)S(1)} copy(f32[128,4,32,16]{2,3,1,0:T(8,128)} %fusion.19) | data formatting | bytes 2097152 | tf_op jit(solution)/shard_map/tkp,skrcp->strcp/dot_general | solution.py:84
  42.1 4.6 %all_gather.9 = bf16[2,1,4,32,128]{4,3,2,1,0:T(8,128)(2,1)S(1)} all-gather(bf16[1,1,4,32,128]{4,3,2,1,0:T(8,128)(2,1)S(1)} %slice.550), channel_id=1, replica_groups=mesh['tm'=2,'rows'=4,'dp'=4] {'tm'}, dimensions={0}, use_global_device_ids=true | all-gather | bytes 98304 | tf_op jit(solution)/shard_map/all_gather | solution.py:91
  47.0 4.2 %collective-permute-start.2 = (bf16[1,16,1,32,128]{4,3,2,1,0:T(8,128)(2,1)S(1)}, bf16[1,16,1,32,128]{4,3,2,1,0:T(8,128)(2,1)S(1)}, u32[]{:S(2)}, u32[]{:S(2)}) collective-permute-start(bf16[1,16,1,32,128]{4,3,2,1,0:T(8,128)(2,1)S(1)} %get-tuple-element.67), channel_id=1, source_target_pairs={{0,4},{4,8},{8,12},{1,5},{5,9},{9,13},{2,6},{6,10},{10,14},{3,7},{... | collective-permute-start | bytes 393224 | tf_op jit(solution)/shard_map/ppermute | solution.py:16
  51.2 1.5 collective-permute-start.3
  52.7 1.1 slice.347
  53.9 4.2 %collective-permute-done.3 = bf16[1,16,1,32,128]{4,3,2,1,0:T(8,128)(2,1)S(1)} collective-permute-done((bf16[1,16,1,32,128]{4,3,2,1,0:T(8,128)(2,1)S(1)}, bf16[1,16,1,32,128]{4,3,2,1,0:T(8,128)(2,1)S(1)}, u32[]{:S(2)}, u32[]{:S(2)}) %collective-permute-start.3) | collective-permute-done | bytes 131104 | tf_op jit(solution)/shard_map/ppermute | solution.py:18
  62.9 1.8 fusion.6
  74.2 40.4 %psum.30 = f32[128]{0:T(128)S(1)} all-reduce(f32[128]{0:T(128)S(1)} %get-tuple-element.26), channel_id=1, replica_groups=mesh['tm'=2,'rows'=4,'dp'=4] {'tm','rows','dp'}, use_global_device_ids=true, to_apply=%region_5.6 | all-reduce | flops 128 | bytes 1024 | tf_op jit(solution)/shard_map/psum | solution.py:138
  115.1 2.2 collective-permute-start.4
  117.3 1.5 collective-permute-start.5
  122.4 1.9 collective-permute-done.5
  127.9 1.3 fusion.1
  129.2 5.4 %copy.172 = f32[16,4,32,128]{2,0,1,3:T(8,128)} copy(f32[16,4,32,128]{3,2,1,0:T(8,128)} %bitcast.442) | data formatting | bytes 2097152 | tf_op jit(solution)/shard_map/reshape.7
  134.6 8.1 %fusion.17 = f32[128,4,32,16]{2,3,1,0:T(8,128)} fusion(f32[16,4,32,128]{2,0,1,3:T(8,128)} %copy.172, f32[16,128]{0,1:T(8,128)S(1)} %copy.167, pred[16,16]{0,1:T(8,128)(4,1)S(1)} %iota_compare_fusion.2), kind=kOutput, calls=%fused_computation.72 | convolution fusion | flops 50429952 | bytes 2105600 | tf_op jit(solution)/shard_map/tkp,strcp->skrcp/dot_general | solution.py:111
  142.8 4.5 %copy.173 = f32[128,4,32,16]{0,2,1,3:T(8,128)} copy(f32[128,4,32,16]{2,3,1,0:T(8,128)} %fusion.17) | data formatting | bytes 2097152 | tf_op jit(solution)/shard_map/tkp,strcp->skrcp/dot_general | solution.py:111
  148.2 5.1 %all_gather.11 = bf16[2,1,4,32,128]{4,3,2,1,0:T(8,128)(2,1)S(1)} all-gather(bf16[1,1,4,32,128]{4,3,2,1,0:T(8,128)(2,1)S(1)} %fusion.71), channel_id=1, replica_groups=mesh['tm'=2,'rows'=4,'dp'=4] {'tm'}, dimensions={0}, use_global_device_ids=true | all-gather | bytes 98304 | tf_op jit(solution)/shard_map/all_gather | solution.py:115
  153.3 1.9 fusion.16
  161.6 57.8 %psum.31 = f32[16,128]{0,1:T(8,128)S(1)} all-reduce(f32[16,128]{0,1:T(8,128)S(1)} %copy.212), channel_id=1, replica_groups=mesh['tm'=2,'rows'=4,'dp'=4] {'rows','dp'}, use_global_device_ids=true, to_apply=%region_7.8 | all-reduce | flops 2048 | bytes 16384 | tf_op jit(solution)/shard_map/psum | solution.py:133
  219.4 1.3 collective-permute-start.6
  220.7 1.3 collective-permute-start.7
  225.4 2.2 collective-permute-done.7
  231.8 1.0 add_convert_fusion
  232.8 124.3 %all-reduce.7.cloned.1.call-done = (f32[3,3,128,128]{3,2,1,0:T(8,128)}, f32[3,3,128,128]{3,2,1,0:T(8,128)}) async-done(((f32[3,3,128,128]{3,2,1,0:T(8,128)}, f32[3,3,128,128]{3,2,1,0:T(8,128)}), (f32[3,3,128,128]{3,2,1,0:T(8,128)}, f32[3,3,128,128]{3,2,1,0:T(8,128)})) %all-reduce.7.cloned.1.call-update) | async-done | bytes 1179664 | tf_op jit(solution)/shard_map/psum | solution.py:138
  357.2 1.9 broadcast_multiply_fusion.1
  359.1 1.9 broadcast_multiply_fusion
  (126 shorter events, 42.2 us)
Async XLA Ops:
  7.2 350.0 %all-reduce.7.cloned.1.call-start = ((), (), s32[]{:S(2)}) async-start(), calls=%async_computation | async-start | bytes 2359296 | tf_op jit(solution)/shard_map/psum | solution.py:138
  8.2 11.5 %collective-permute-start = (bf16[1,16,1,32,128]{4,3,2,1,0:T(8,128)(2,1)S(1)}, bf16[1,16,1,32,128]{4,3,2,1,0:T(8,128)(2,1)S(1)}, u32[]{:S(2)}, u32[]{:S(2)}) collective-permute-start(bf16[1,16,1,32,128]{4,3,2,1,0:T(8,128)(2,1)S(1)} %get-tuple-element.71), channel_id=1, source_target_pairs={{0,4},{4,8},{8,12},{1,5},{5,9},{9,13},{2,6},{6,10},{10,14},{3,7},{... | collective-permute-start | bytes 393224 | tf_op jit(solution)/shard_map/ppermute | solution.py:16
  13.2 6.9 %collective-permute-start.1 = (bf16[1,16,1,32,128]{4,3,2,1,0:T(8,128)(2,1)S(1)}, bf16[1,16,1,32,128]{4,3,2,1,0:T(8,128)(2,1)S(1)}, u32[]{:S(2)}, u32[]{:S(2)}) collective-permute-start(bf16[1,16,1,32,128]{4,3,2,1,0:T(8,128)(2,1)S(1)} %get-tuple-element.72), channel_id=1, source_target_pairs={{4,0},{8,4},{12,8},{5,1},{9,5},{13,9},{6,2},{10,6},{14,10},{7,3},{... | collective-permute-start | bytes 393224 | tf_op jit(solution)/shard_map/ppermute | solution.py:18
  21.7 1.0 copy-start.6
  22.3 1.1 copy-start
  23.4 0.8 copy-start.3
  23.4 1.9 copy-start.1
  42.1 10.6 %copy-start.10 = (f32[16,128]{1,0:T(8,128)S(1)}, f32[16,128]{1,0:T(8,128)}, u32[]{:S(2)}) copy-start(f32[16,128]{1,0:T(8,128)} %param.11) | copy-start | bytes 24580
  47.0 6.9 %collective-permute-start.2 = (bf16[1,16,1,32,128]{4,3,2,1,0:T(8,128)(2,1)S(1)}, bf16[1,16,1,32,128]{4,3,2,1,0:T(8,128)(2,1)S(1)}, u32[]{:S(2)}, u32[]{:S(2)}) collective-permute-start(bf16[1,16,1,32,128]{4,3,2,1,0:T(8,128)(2,1)S(1)} %get-tuple-element.67), channel_id=1, source_target_pairs={{0,4},{4,8},{8,12},{1,5},{5,9},{9,13},{2,6},{6,10},{10,14},{3,7},{... | collective-permute-start | bytes 393224 | tf_op jit(solution)/shard_map/ppermute | solution.py:16
  51.2 6.9 %collective-permute-start.3 = (bf16[1,16,1,32,128]{4,3,2,1,0:T(8,128)(2,1)S(1)}, bf16[1,16,1,32,128]{4,3,2,1,0:T(8,128)(2,1)S(1)}, u32[]{:S(2)}, u32[]{:S(2)}) collective-permute-start(bf16[1,16,1,32,128]{4,3,2,1,0:T(8,128)(2,1)S(1)} %get-tuple-element.68), channel_id=1, source_target_pairs={{4,0},{8,4},{12,8},{5,1},{9,5},{13,9},{6,2},{10,6},{14,10},{7,3},{... | collective-permute-start | bytes 393224 | tf_op jit(solution)/shard_map/ppermute | solution.py:18
  58.6 1.0 copy-start.5
  61.9 1.0 copy-start.8
  61.9 1.0 copy-start.11
  115.1 7.3 %collective-permute-start.4 = (bf16[1,16,1,32,128]{4,3,2,1,0:T(8,128)(2,1)}, bf16[1,16,1,32,128]{4,3,2,1,0:T(8,128)(2,1)S(1)}, u32[]{:S(2)}, u32[]{:S(2)}) collective-permute-start(bf16[1,16,1,32,128]{4,3,2,1,0:T(8,128)(2,1)} %get-tuple-element.63), channel_id=1, source_target_pairs={{0,4},{4,8},{8,12},{1,5},{5,9},{9,13},{2,6},{6,10},{10,14},{3,7},{... | collective-permute-start | bytes 393224 | tf_op jit(solution)/shard_map/ppermute | solution.py:16
  117.3 7.1 %collective-permute-start.5 = (bf16[1,16,1,32,128]{4,3,2,1,0:T(8,128)(2,1)}, bf16[1,16,1,32,128]{4,3,2,1,0:T(8,128)(2,1)S(1)}, u32[]{:S(2)}, u32[]{:S(2)}) collective-permute-start(bf16[1,16,1,32,128]{4,3,2,1,0:T(8,128)(2,1)} %get-tuple-element.64), channel_id=1, source_target_pairs={{4,0},{8,4},{12,8},{5,1},{9,5},{13,9},{6,2},{10,6},{14,10},{7,3},{... | collective-permute-start | bytes 393224 | tf_op jit(solution)/shard_map/ppermute | solution.py:18
  147.3 7.9 %copy-start.2 = (bf16[1,16,4,32,128]{4,3,2,1,0:T(8,128)(2,1)S(1)}, bf16[1,16,4,32,128]{4,3,2,1,0:T(8,128)(2,1)}, u32[]{:S(2)}) copy-start(bf16[1,16,4,32,128]{4,3,2,1,0:T(8,128)(2,1)} %copy-done.1) | copy-start | bytes 1572868
  153.3 2.3 copy-start.4
  160.5 61.5 %copy-start.9 = (f32[1,128,128]{2,1,0:T(8,128)S(1)}, f32[1,128,128]{2,1,0:T(8,128)}, u32[]{:S(2)}) copy-start(f32[1,128,128]{2,1,0:T(8,128)} %convolution_bitcast_fusion.14) | copy-start | bytes 196612
  219.4 6.0 %collective-permute-start.6 = (bf16[1,16,1,32,128]{4,3,2,1,0:T(8,128)(2,1)S(1)}, bf16[1,16,1,32,128]{4,3,2,1,0:T(8,128)(2,1)S(1)}, u32[]{:S(2)}, u32[]{:S(2)}) collective-permute-start(bf16[1,16,1,32,128]{4,3,2,1,0:T(8,128)(2,1)S(1)} %get-tuple-element.59), channel_id=1, source_target_pairs={{0,4},{4,8},{8,12},{1,5},{5,9},{9,13},{2,6},{6,10},{10,14},{3,7},{... | collective-permute-start | bytes 393224 | tf_op jit(solution)/shard_map/ppermute | solution.py:16
  220.7 6.9 %collective-permute-start.7 = (bf16[1,16,1,32,128]{4,3,2,1,0:T(8,128)(2,1)S(1)}, bf16[1,16,1,32,128]{4,3,2,1,0:T(8,128)(2,1)S(1)}, u32[]{:S(2)}, u32[]{:S(2)}) collective-permute-start(bf16[1,16,1,32,128]{4,3,2,1,0:T(8,128)(2,1)S(1)} %get-tuple-element.60), channel_id=1, source_target_pairs={{4,0},{8,4},{12,8},{5,1},{9,5},{13,9},{6,2},{10,6},{14,10},{7,3},{... | collective-permute-start | bytes 393224 | tf_op jit(solution)/shard_map/ppermute | solution.py:18
  228.0 1.0 copy-start.7
Sparse Core Ops, SparseCore 0:
  225.5 131.6 all-reduce.6
where the time goes:
time: 369 us; the launch traced here: 368 us
  waiting for transfers between devices  133 us (36%)
  blocking collectives  112 us (30%)
  matrix products  42.6 us (12%)
  local copies, waits for them, and re-layouts  26.5 us (7%)
  other arithmetic  20.8 us (6%)
  starting transfers between devices  18.3 us (5%)
  between operations  14.6 us (4%)
    psum x1, waiting for transfers between devices, on_device(): lax.psum((in_grad, out_grad, gain_grad), ('tm', 'rows', 'dp'))  124 us
    psum x1, blocking collectives, on_device(): decay_grad = lax.psum(decay_part, ('rows', 'dp')) * decay_scale  57.8 us
    psum x1, blocking collectives, on_device(): lax.psum((in_grad, out_grad, gain_grad), ('tm', 'rows', 'dp'))  40.4 us
    dot_general x18, matrix products, kernel_grad(): lax.dot_general(piece, flat_grad, (((0,), (0,)), ((), ())), preferred_ele...  14.9 us
    ppermute x4, starting transfers between devices, padded_2(): lax.ppermute(tail, axis, [(i, (i + 1) % count) for i in range(ends)])  12.7 us
    ppermute x4, waiting for transfers between devices, padded_2(): lax.ppermute(head, axis, [((i + 1) % count, i) for i in range(ends)])  8.64 us
    dot_general x1, matrix products, on_device(): jnp.einsum('tkp,skrcp->strcp', within, drive, precision=lax.Precision.HIG...  8.27 us
    dot_general x1, matrix products, on_device(): jnp.einsum('tkp,strcp->skrcp', within, state_grad, precision=lax.Precisio...  8.14 us
  transfers between devices with their start and end apart: 9, of which 5 were waited for; matrix products, arithmetic and copies ran while one was open for 4% of the time, Pallas kernels for 0%

commit v1 on v0

--- a/solution.py
+++ b/solution.py
@@ -1,8 +1,17 @@
+import functools
 import math
 import jax
 import jax.numpy as jnp
 from jax import lax
 from jax.sharding import PartitionSpec as P
+
+
+def unit_load(state, axis_key):
+    g_now = jnp.sum(lax.all_gather(state, axis_name=axis_key), axis=0)
+    return g_now
+
+
+play_set = functools.partial(unit_load, axis_key=("rows", "dp"))
 
 
 def padded_2(cells, sides, width):
@@ -130,7 +139,7 @@
         adjoint * jnp.exp(log_decay)[None, :, None, None, :] * previous, axis=(0, 2, 3)
     )
     decay_scale = 1.0 / math.sqrt(seqs * rows * cols * lax.axis_size("rows") * lax.axis_size("dp"))
-    decay_grad = lax.psum(decay_part, ("rows", "dp")) * decay_scale
+    decay_grad = play_set(decay_part) * decay_scale
     adjoint_bf = adjoint.astype(jnp.bfloat16)
     in_grad = kernel_grad(padded_x, adjoint_bf)
     padded_a = pad_columns(padded_2(adjoint_bf, (("rows", 2),), 1))

time: 369 us -> 331 us (0.90)
  blocking collectives: 112 us -> 75.9 us
    psum x1 -> x0, blocking collectives: 57.8 us -> none  [on_device(): decay_grad = lax.psum(decay_part, ('rows', 'dp')) * decay_scale]
    all_gather x0 -> x1, blocking collectives: none -> 21.7 us  [unit_load(): g_now = jnp.sum(lax.all_gather(state, axis_name=axis_key), axis=0)]
where the time goes in v1:
time: 331 us; the launch traced here: 330 us
  waiting for transfers between devices  131 us (40%)
  blocking collectives  75.9 us (23%)
  matrix products  42.6 us (13%)
  local copies, waits for them, and re-layouts  25.7 us (8%)
  other arithmetic  21.4 us (6%)
  starting transfers between devices  18.3 us (6%)
  between operations  14.6 us (4%)
    psum x1, waiting for transfers between devices, on_device(): lax.psum((in_grad, out_grad, gain_grad), ('tm', 'rows', 'dp'))  122 us
    psum x1, blocking collectives, on_device(): lax.psum((in_grad, out_grad, gain_grad), ('tm', 'rows', 'dp'))  40.4 us
    all_gather x1, blocking collectives, unit_load(): g_now = jnp.sum(lax.all_gather(state, axis_name=axis_key), axis=0)  21.7 us
    dot_general x18, matrix products, kernel_grad(): lax.dot_general(piece, flat_grad, (((0,), (0,)), ((), ())), preferred_ele...  14.9 us
    ppermute x4, starting transfers between devices, padded_2(): lax.ppermute(tail, axis, [(i, (i + 1) % count) for i in range(ends)])  12.7 us
    ppermute x4, waiting for transfers between devices, padded_2(): lax.ppermute(head, axis, [((i + 1) % count, i) for i in range(ends)])  9.49 us
    dot_general x1, matrix products, on_device(): jnp.einsum('tkp,skrcp->strcp', within, drive, precision=lax.Precision.HIG...  8.27 us
    dot_general x1, matrix products, on_device(): jnp.einsum('tkp,strcp->skrcp', within, state_grad, precision=lax.Precisio...  8.14 us
  transfers between devices with their start and end apart: 9, of which 5 were waited for; matrix products, arithmetic and copies ran while one was open for 4% of the time, Pallas kernels for 0%

profile of v1, /device:TPU:0, one launch (start us, length us, event | category | flops | bytes accessed | tf_op | source)
XLA Modules:
  0.0 329.6 jit_solution(17517662137105779410)
XLA Ops:
  7.2 1.0 fusion.177
  8.2 5.0 %collective-permute-start = (bf16[1,16,1,32,128]{4,3,2,1,0:T(8,128)(2,1)S(1)}, bf16[1,16,1,32,128]{4,3,2,1,0:T(8,128)(2,1)S(1)}, u32[]{:S(2)}, u32[]{:S(2)}) collective-permute-start(bf16[1,16,1,32,128]{4,3,2,1,0:T(8,128)(2,1)S(1)} %get-tuple-element.53), channel_id=1, source_target_pairs={{0,4},{4,8},{8,12},{1,5},{5,9},{9,13},{2,6},{6,10},{10,14},{3,7},{... | collective-permute-start | bytes 393224 | tf_op jit(solution)/shard_map/ppermute | solution.py:25
  13.2 1.3 collective-permute-start.1
  15.2 4.2 %all-gather.1 = f32[2,1,128]{2,1,0:T(1,128)S(1)} all-gather(f32[1,1,128]{2,1,0:T(1,128)S(1)} %slice_bitcast_fusion.1), channel_id=1, replica_groups=mesh['tm'=2,'rows'=4,'dp'=4] {'tm'}, dimensions={0}, use_global_device_ids=true | all-gather | bytes 1536 | tf_op jit(solution)/shard_map/all_gather | solution.py:96
  20.0 1.6 fusion.25
  25.6 4.5 %copy.250 = f32[16,4,32,128]{2,0,1,3:T(8,128)} copy(f32[16,4,32,128]{3,2,1,0:T(8,128)S(1)} %bitcast.444) | data formatting | bytes 2097152 | tf_op jit(solution)/shard_map/reshape
  30.1 8.3 %fusion.19 = f32[128,4,32,16]{2,3,1,0:T(8,128)} fusion(f32[16,4,32,128]{2,0,1,3:T(8,128)} %copy.250, f32[16,128]{0,1:T(8,128)S(1)} %copy.248, pred[16,16]{0,1:T(8,128)(4,1)S(1)} %iota_compare_fusion.2), kind=kOutput, calls=%fused_computation.74 | convolution fusion | flops 50429952 | bytes 2105600 | tf_op jit(solution)/shard_map/tkp,skrcp->strcp/dot_general | solution.py:93
  38.4 3.7 %copy.252 = f32[128,4,32,16]{0,2,1,3:T(8,128)S(1)} copy(f32[128,4,32,16]{2,3,1,0:T(8,128)} %fusion.19) | data formatting | bytes 2097152 | tf_op jit(solution)/shard_map/tkp,skrcp->strcp/dot_general | solution.py:93
  42.1 4.6 %all_gather.15 = bf16[2,1,4,32,128]{4,3,2,1,0:T(8,128)(2,1)S(1)} all-gather(bf16[1,1,4,32,128]{4,3,2,1,0:T(8,128)(2,1)S(1)} %slice.550), channel_id=1, replica_groups=mesh['tm'=2,'rows'=4,'dp'=4] {'tm'}, dimensions={0}, use_global_device_ids=true | all-gather | bytes 98304 | tf_op jit(solution)/shard_map/all_gather | solution.py:100
  47.0 4.2 %collective-permute-start.2 = (bf16[1,16,1,32,128]{4,3,2,1,0:T(8,128)(2,1)S(1)}, bf16[1,16,1,32,128]{4,3,2,1,0:T(8,128)(2,1)S(1)}, u32[]{:S(2)}, u32[]{:S(2)}) collective-permute-start(bf16[1,16,1,32,128]{4,3,2,1,0:T(8,128)(2,1)S(1)} %get-tuple-element.49), channel_id=1, source_target_pairs={{0,4},{4,8},{8,12},{1,5},{5,9},{9,13},{2,6},{6,10},{10,14},{3,7},{... | collective-permute-start | bytes 393224 | tf_op jit(solution)/shard_map/ppermute | solution.py:25
  51.2 1.5 collective-permute-start.3
  52.7 1.1 slice.347
  53.9 4.2 %collective-permute-done.3 = bf16[1,16,1,32,128]{4,3,2,1,0:T(8,128)(2,1)S(1)} collective-permute-done((bf16[1,16,1,32,128]{4,3,2,1,0:T(8,128)(2,1)S(1)}, bf16[1,16,1,32,128]{4,3,2,1,0:T(8,128)(2,1)S(1)}, u32[]{:S(2)}, u32[]{:S(2)}) %collective-permute-start.3) | collective-permute-done | bytes 131104 | tf_op jit(solution)/shard_map/ppermute | solution.py:27
  62.9 1.8 fusion.6
  74.2 40.4 %psum.23 = f32[128]{0:T(128)S(1)} all-reduce(f32[128]{0:T(128)S(1)} %get-tuple-element.8), channel_id=1, replica_groups=mesh['tm'=2,'rows'=4,'dp'=4] {'tm','rows','dp'}, use_global_device_ids=true, to_apply=%region_5.6 | all-reduce | flops 128 | bytes 1024 | tf_op jit(solution)/shard_map/psum | solution.py:147
  115.1 2.2 collective-permute-start.4
  117.3 1.5 collective-permute-start.5
  122.4 1.9 collective-permute-done.5
  127.9 1.3 fusion.1
  129.2 5.4 %copy.253 = f32[16,4,32,128]{2,0,1,3:T(8,128)} copy(f32[16,4,32,128]{3,2,1,0:T(8,128)} %bitcast.443) | data formatting | bytes 2097152 | tf_op jit(solution)/shard_map/reshape.7
  134.6 8.1 %fusion.17 = f32[128,4,32,16]{2,3,1,0:T(8,128)} fusion(f32[16,4,32,128]{2,0,1,3:T(8,128)} %copy.253, f32[16,128]{0,1:T(8,128)S(1)} %copy.248, pred[16,16]{0,1:T(8,128)(4,1)S(1)} %iota_compare_fusion.2), kind=kOutput, calls=%fused_computation.72 | convolution fusion | flops 50429952 | bytes 2105600 | tf_op jit(solution)/shard_map/tkp,strcp->skrcp/dot_general | solution.py:120
  142.8 4.5 %copy.254 = f32[128,4,32,16]{0,2,1,3:T(8,128)} copy(f32[128,4,32,16]{2,3,1,0:T(8,128)} %fusion.17) | data formatting | bytes 2097152 | tf_op jit(solution)/shard_map/tkp,strcp->skrcp/dot_general | solution.py:120
  148.2 5.1 %all_gather.17 = bf16[2,1,4,32,128]{4,3,2,1,0:T(8,128)(2,1)S(1)} all-gather(bf16[1,1,4,32,128]{4,3,2,1,0:T(8,128)(2,1)S(1)} %fusion.71), channel_id=1, replica_groups=mesh['tm'=2,'rows'=4,'dp'=4] {'tm'}, dimensions={0}, use_global_device_ids=true | all-gather | bytes 98304 | tf_op jit(solution)/shard_map/all_gather | solution.py:124
  153.3 1.9 fusion.16
  161.5 21.7 %all-gather = f32[256,128]{1,0:T(8,128)S(1)} all-gather(f32[16,128]{1,0:T(8,128)S(1)} %get-tuple-element.13), channel_id=2, replica_groups=mesh['tm'=2,'rows'=4,'dp'=4] {'rows','dp'}, dimensions={0}, use_global_device_ids=true | all-gather | bytes 139264 | tf_op jit(solution)/shard_map/all_gather | solution.py:10
  183.2 1.3 collective-permute-start.6
  184.5 1.3 collective-permute-start.7
  189.1 3.0 collective-permute-done.7
  196.3 1.0 add_convert_fusion
  197.4 121.6 %all-reduce.7.cloned.1.call-done = (f32[3,3,128,128]{3,2,1,0:T(8,128)}, f32[3,3,128,128]{3,2,1,0:T(8,128)}) async-done(((f32[3,3,128,128]{3,2,1,0:T(8,128)}, f32[3,3,128,128]{3,2,1,0:T(8,128)}), (f32[3,3,128,128]{3,2,1,0:T(8,128)}, f32[3,3,128,128]{3,2,1,0:T(8,128)})) %all-reduce.7.cloned.1.call-update) | async-done | bytes 1179664 | tf_op jit(solution)/shard_map/psum | solution.py:147
  319.0 1.9 broadcast_multiply_fusion.1
  320.9 1.9 broadcast_multiply_fusion
  (125 shorter events, 42.0 us)
Async XLA Ops:
  7.2 311.8 %all-reduce.7.cloned.1.call-start = ((), (), s32[]{:S(2)}) async-start(), calls=%async_computation | async-start | bytes 2359296 | tf_op jit(solution)/shard_map/psum | solution.py:147
  8.2 11.5 %collective-permute-start = (bf16[1,16,1,32,128]{4,3,2,1,0:T(8,128)(2,1)S(1)}, bf16[1,16,1,32,128]{4,3,2,1,0:T(8,128)(2,1)S(1)}, u32[]{:S(2)}, u32[]{:S(2)}) collective-permute-start(bf16[1,16,1,32,128]{4,3,2,1,0:T(8,128)(2,1)S(1)} %get-tuple-element.53), channel_id=1, source_target_pairs={{0,4},{4,8},{8,12},{1,5},{5,9},{9,13},{2,6},{6,10},{10,14},{3,7},{... | collective-permute-start | bytes 393224 | tf_op jit(solution)/shard_map/ppermute | solution.py:25
  13.2 6.9 %collective-permute-start.1 = (bf16[1,16,1,32,128]{4,3,2,1,0:T(8,128)(2,1)S(1)}, bf16[1,16,1,32,128]{4,3,2,1,0:T(8,128)(2,1)S(1)}, u32[]{:S(2)}, u32[]{:S(2)}) collective-permute-start(bf16[1,16,1,32,128]{4,3,2,1,0:T(8,128)(2,1)S(1)} %get-tuple-element.54), channel_id=1, source_target_pairs={{4,0},{8,4},{12,8},{5,1},{9,5},{13,9},{6,2},{10,6},{14,10},{7,3},{... | collective-permute-start | bytes 393224 | tf_op jit(solution)/shard_map/ppermute | solution.py:27
  21.7 1.0 copy-start.6
  22.3 1.1 copy-start
  23.4 0.8 copy-start.3
  23.4 1.9 copy-start.1
  42.1 10.6 %copy-start.10 = (f32[16,128]{1,0:T(8,128)S(1)}, f32[16,128]{1,0:T(8,128)}, u32[]{:S(2)}) copy-start(f32[16,128]{1,0:T(8,128)} %param.11) | copy-start | bytes 24580
  47.0 6.9 %collective-permute-start.2 = (bf16[1,16,1,32,128]{4,3,2,1,0:T(8,128)(2,1)S(1)}, bf16[1,16,1,32,128]{4,3,2,1,0:T(8,128)(2,1)S(1)}, u32[]{:S(2)}, u32[]{:S(2)}) collective-permute-start(bf16[1,16,1,32,128]{4,3,2,1,0:T(8,128)(2,1)S(1)} %get-tuple-element.49), channel_id=1, source_target_pairs={{0,4},{4,8},{8,12},{1,5},{5,9},{9,13},{2,6},{6,10},{10,14},{3,7},{... | collective-permute-start | bytes 393224 | tf_op jit(solution)/shard_map/ppermute | solution.py:25
  51.2 6.9 %collective-permute-start.3 = (bf16[1,16,1,32,128]{4,3,2,1,0:T(8,128)(2,1)S(1)}, bf16[1,16,1,32,128]{4,3,2,1,0:T(8,128)(2,1)S(1)}, u32[]{:S(2)}, u32[]{:S(2)}) collective-permute-start(bf16[1,16,1,32,128]{4,3,2,1,0:T(8,128)(2,1)S(1)} %get-tuple-element.50), channel_id=1, source_target_pairs={{4,0},{8,4},{12,8},{5,1},{9,5},{13,9},{6,2},{10,6},{14,10},{7,3},{... | collective-permute-start | bytes 393224 | tf_op jit(solution)/shard_map/ppermute | solution.py:27
  58.6 1.0 copy-start.5
  61.9 1.0 copy-start.8
  61.9 1.0 copy-start.11
  115.1 7.3 %collective-permute-start.4 = (bf16[1,16,1,32,128]{4,3,2,1,0:T(8,128)(2,1)}, bf16[1,16,1,32,128]{4,3,2,1,0:T(8,128)(2,1)S(1)}, u32[]{:S(2)}, u32[]{:S(2)}) collective-permute-start(bf16[1,16,1,32,128]{4,3,2,1,0:T(8,128)(2,1)} %get-tuple-element.45), channel_id=1, source_target_pairs={{0,4},{4,8},{8,12},{1,5},{5,9},{9,13},{2,6},{6,10},{10,14},{3,7},{... | collective-permute-start | bytes 393224 | tf_op jit(solution)/shard_map/ppermute | solution.py:25
  117.3 7.1 %collective-permute-start.5 = (bf16[1,16,1,32,128]{4,3,2,1,0:T(8,128)(2,1)}, bf16[1,16,1,32,128]{4,3,2,1,0:T(8,128)(2,1)S(1)}, u32[]{:S(2)}, u32[]{:S(2)}) collective-permute-start(bf16[1,16,1,32,128]{4,3,2,1,0:T(8,128)(2,1)} %get-tuple-element.46), channel_id=1, source_target_pairs={{4,0},{8,4},{12,8},{5,1},{9,5},{13,9},{6,2},{10,6},{14,10},{7,3},{... | collective-permute-start | bytes 393224 | tf_op jit(solution)/shard_map/ppermute | solution.py:27
  147.3 7.9 %copy-start.2 = (bf16[1,16,4,32,128]{4,3,2,1,0:T(8,128)(2,1)S(1)}, bf16[1,16,4,32,128]{4,3,2,1,0:T(8,128)(2,1)}, u32[]{:S(2)}) copy-start(bf16[1,16,4,32,128]{4,3,2,1,0:T(8,128)(2,1)} %copy-done.1) | copy-start | bytes 1572868
  153.3 2.3 copy-start.4
  160.5 25.3 %copy-start.9 = (f32[1,128,128]{2,1,0:T(8,128)S(1)}, f32[1,128,128]{2,1,0:T(8,128)}, u32[]{:S(2)}) copy-start(f32[1,128,128]{2,1,0:T(8,128)} %convolution_bitcast_fusion.14) | copy-start | bytes 196612
  183.2 5.9 %collective-permute-start.6 = (bf16[1,16,1,32,128]{4,3,2,1,0:T(8,128)(2,1)S(1)}, bf16[1,16,1,32,128]{4,3,2,1,0:T(8,128)(2,1)S(1)}, u32[]{:S(2)}, u32[]{:S(2)}) collective-permute-start(bf16[1,16,1,32,128]{4,3,2,1,0:T(8,128)(2,1)S(1)} %get-tuple-element.41), channel_id=1, source_target_pairs={{0,4},{4,8},{8,12},{1,5},{5,9},{9,13},{2,6},{6,10},{10,14},{3,7},{... | collective-permute-start | bytes 393224 | tf_op jit(solution)/shard_map/ppermute | solution.py:25
  184.5 7.6 %collective-permute-start.7 = (bf16[1,16,1,32,128]{4,3,2,1,0:T(8,128)(2,1)S(1)}, bf16[1,16,1,32,128]{4,3,2,1,0:T(8,128)(2,1)S(1)}, u32[]{:S(2)}, u32[]{:S(2)}) collective-permute-start(bf16[1,16,1,32,128]{4,3,2,1,0:T(8,128)(2,1)S(1)} %get-tuple-element.42), channel_id=1, source_target_pairs={{4,0},{8,4},{12,8},{5,1},{9,5},{13,9},{6,2},{10,6},{14,10},{7,3},{... | collective-permute-start | bytes 393224 | tf_op jit(solution)/shard_map/ppermute | solution.py:27
  192.6 1.0 copy-start.7
Sparse Core Ops, SparseCore 0:
  188.6 130.3 all-reduce.6
